TPU v7x, 256 devices: a whole 4x4x8 slice. The times are simulated.
256 devices in a mesh: dp: 128 (over y, z, x), grp: 2 (over core).
Axes of the slice: x: 4, y: 4, z: 8, core: 2. Of those that a mesh axis runs over, the one named last changes fastest.
Arguments:
- embeddings: bfloat16 [65536, 1024], P(('dp', 'grp')), may hold values from -6 to 6
- owner_dest: int32 [65536, 1], P(('dp', 'grp')), may hold values from 0 to 127; in each aligned block of 256 rows (0 to 255, 256 to 511, ...) at most 6 rows name the same one
- cluster_slot: int32 [65536, 1], P(('dp', 'grp')), may hold values from 0 to 7
- cluster_rank: int32 [1024], replicated, may hold values from 0 to 1023, each once
- centroids: bfloat16 [1024, 1024], P('dp'), may hold values from -2 to 2
Outputs:
- shift: bfloat16 [1024, 1792], replicated
- moment: float32 [1024, 256, 256], P(('dp', 'grp'))
Inputs may be any that keep to these rules, and one draw needn't show every extreme that they name: `owner_dest`: among the rows of one device (aligned blocks of 256 rows), no owner is named by more than 6 rows, a bound that some block reaches. `cluster_rank`: A permutation.
All inputs are finite; a program needn't handle non-finite values.
Results may differ from a plain program's by a relative error of at most 0.0034.
Values may be sent and summed in bfloat16 or wider, within the bound.
A program may use at most 64 MiB of HBM per device.

v0:
```python
import jax
import jax.numpy as jnp
from jax import lax
from jax.sharding import PartitionSpec as P

D = 1024
D_SMALL = 256
D_MID = 512


def residuals(rows, cent):
    rows = rows.astype(jnp.float32)
    pieces = []
    for width in (D_SMALL, D_MID, D):
        part = rows[:, :width]
        scale = lax.rsqrt(jnp.mean(part * part, axis=-1, keepdims=True) + 1e-06)
        pieces.append(part * scale - cent[:, :width])
    return jnp.concatenate(pieces, axis=1).astype(jnp.bfloat16)


def slot_onehot(slots, per_owner):
    return (slots[:, None] == jnp.arange(per_owner, dtype=jnp.int32)[None, :]).astype(jnp.bfloat16)


def moments(select, small):
    count_rows = small.shape[0]
    per_owner = select.shape[1]
    spread = (select[:, :, None] * small[:, None, :]).reshape(count_rows, per_owner * D_SMALL)
    gram = jnp.einsum("sa,sb->ab", spread, small, preferred_element_type=jnp.float32)
    return gram.reshape(per_owner, D_SMALL, D_SMALL)


def on_device(embeddings, owner_dest, cluster_slot, cluster_rank, centroids):
    rows_here = embeddings.shape[0]
    width = embeddings.shape[1]
    owners = lax.axis_size("dp")
    per_owner = centroids.shape[0]
    capacity = 3 * rows_here // owners
    dest = owner_dest[:, 0]
    slot = cluster_slot[:, 0]
    hits = (dest[:, None] == jnp.arange(owners, dtype=jnp.int32)[None, :]).astype(jnp.int32)
    before = jnp.cumsum(hits, axis=0) - hits
    position = jnp.sum(before * hits, axis=1)
    target = dest * capacity + position

    def pack(values, fill):
        buffer = jnp.full((owners * capacity,) + values.shape[1:], fill, values.dtype)
        buffer = buffer.at[target].set(values)
        return buffer.reshape((owners, capacity) + values.shape[1:])

    sent_ids = pack(slot, -1)
    sent_rows = pack(embeddings, 0)
    got_rows = lax.all_to_all(sent_rows, "dp", split_axis=0, concat_axis=0, tiled=True)
    got_ids = lax.all_to_all(sent_ids, "dp", split_axis=0, concat_axis=0, tiled=True)
    lead = got_rows.shape[0]
    middle = got_rows.shape[1]
    flat_ids = got_ids.reshape(-1)
    select = slot_onehot(flat_ids, per_owner)
    cent = jnp.dot(select, centroids, preferred_element_type=jnp.float32)
    resid = residuals(got_rows.reshape(-1, width), cent)
    resid, got_ids = (resid.reshape(lead, middle, resid.shape[1]), got_ids)
    resid = resid.reshape(-1, resid.shape[2])
    select = slot_onehot(got_ids.reshape(-1), per_owner)
    sums = jnp.einsum("sc,sw->cw", select, resid, preferred_element_type=jnp.float32)
    counts = jnp.sum(select.astype(jnp.float32), axis=0)
    gram = moments(select, resid[:, :D_SMALL])
    sums_part, counts_part, gram_part = (
        lax.psum_scatter(sums, "grp", scatter_dimension=0, tiled=True),
        lax.psum_scatter(counts, "grp", scatter_dimension=0, tiled=True),
        lax.psum_scatter(gram, "grp", scatter_dimension=0, tiled=True),
    )
    denom = counts_part + 1.0
    table_part = (sums_part / denom[:, None]).astype(jnp.bfloat16)
    table = lax.all_gather(table_part, ("dp", "grp"), axis=0, tiled=True)
    shift = table[cluster_rank]
    moment = gram_part / denom[:, None, None]
    return (shift, moment)


def solution(mesh):
    placed = (
        P(("dp", "grp"), None),
        P(("dp", "grp"), None),
        P(("dp", "grp"), None),
        P(),
        P("dp", None),
    )
    return jax.shard_map(
        on_device,
        mesh=mesh,
        in_specs=placed,
        out_specs=(P(), P(("dp", "grp"), None, None)),
        check_vma=False,
    )
```

profile of v0, /device:TPU:1, one launch (start us, length us, event | category | flops | bytes accessed | tf_op | source)
XLA Modules:
  0.0 256.8 jit_solution(13013240612006386319)
XLA Ops:
  8.0 0.8 copy.12
  9.1 0.9 fusion.18
  10.7 1.6 scatter_custom_fusion
  12.2 0.8 all_to_all.9
  13.0 16.3 %all-to-all-start = ((s32[128,1,6]{2,1,0:T(1,128)}), s32[128,1,6]{2,1,0:T(1,128)S(1)}, u32[]{:S(2)}, u32[]{:S(2)}) async-start(s32[128,1,6]{2,1,0:T(1,128)} %bitcast.8), calls=%async_computation | async-start | bytes 131072 | tf_op jit(solution)/shard_map/all_to_all | solution.py:54
  29.3 2.6 %scatter_custom_fusion.1 = bf16[768,1024]{1,0:T(8,128)(2,1)S(1)} fusion(s32[256]{0:T(256)S(1)} %bitcast.40, bf16[256,1024]{1,0:T(8,128)(2,1)} %param.5, bf16[]{:T(256)} %constant.7.clone.1), kind=kCustom, calls=%fused_computation.22 | custom fusion | bytes 1573376 | tf_op jit(solution)/shard_map/scatter | solution.py:48
  32.0 1.6 reshape.100
  33.5 6.3 %all-to-all-done = s32[128,1,6]{2,1,0:T(1,128)S(1)} async-done(((s32[128,1,6]{2,1,0:T(1,128)}), s32[128,1,6]{2,1,0:T(1,128)S(1)}, u32[]{:S(2)}, u32[]{:S(2)}) %all-to-all-start) | async-done | bytes 3104 | tf_op jit(solution)/shard_map/all_to_all | solution.py:54
  39.8 6.9 %all-to-all-start.1 = ((bf16[128,6,1024]{2,1,0:T(8,128)(2,1)}), bf16[128,6,1024]{2,1,0:T(8,128)(2,1)S(1)}, u32[]{:S(2)}, u32[]{:S(2)}) async-start(bf16[128,6,1024]{2,1,0:T(8,128)(2,1)} %reshape.100), calls=%async_computation.1 | async-start | bytes 4194304 | tf_op jit(solution)/shard_map/all_to_all | solution.py:53
  47.4 0.8 reduce.4
  48.9 47.0 %all-to-all-done.1 = bf16[128,6,1024]{2,1,0:T(8,128)(2,1)S(1)} async-done(((bf16[128,6,1024]{2,1,0:T(8,128)(2,1)}), bf16[128,6,1024]{2,1,0:T(8,128)(2,1)S(1)}, u32[]{:S(2)}, u32[]{:S(2)}) %all-to-all-start.1) | async-done | bytes 1572896 | tf_op jit(solution)/shard_map/all_to_all | solution.py:53
  97.3 2.5 reshape.101
  100.1 1.8 subtract_convert_fusion
  101.9 1.7 copy-done.2
  103.7 0.9 copy.15
  104.7 3.3 %fusion = f32[8,256,256]{2,1,0:T(8,128)} fusion(bf16[768,256]{0,1:T(8,128)(2,1)} %copy.15, bf16[768,8]{0,1:T(8,128)(2,1)} %fusion.22, bf16[768,256]{1,0:T(8,128)(2,1)S(1)} %fusion.12), kind=kOutput, calls=%fused_computation.4 | convolution fusion | flops 806879232 | bytes 2895872 | tf_op jit(solution)/shard_map/sa,sb->ab/dot_general | solution.py:29
  108.1 1.4 dynamic-slice
  109.5 1.3 convert_reduce_fusion
  111.0 1.6 fusion.9
  113.8 7.5 %all-reduce.2 = (f32[8]{0:T(128)S(1)}, f32[8,1792]{1,0:T(8,128)S(1)}) all-reduce(f32[8]{0:T(128)S(1)} %copy-done.7, f32[8,1792]{1,0:T(8,128)S(1)} %fusion.3), channel_id=3, replica_groups=mesh['dp'=128,'grp'=2] {'grp'}, use_global_device_ids=true, to_apply=%region_10.11.clone | all-reduce | flops 14344 | bytes 114752
  122.2 2.4 broadcast_divide_fusion
  124.5 107.6 %all-gather.3.cloned.1.call-done = bf16[256,4,1792]{2,1,0:T(4,128)(2,1)} async-done(((bf16[1,4,1792]{2,1,0:T(4,128)(2,1)}), bf16[256,4,1792]{2,1,0:T(4,128)(2,1)}) %all-gather.3.cloned.1.call-update) | async-done | bytes 3670032 | tf_op jit(solution)/shard_map/all_gather | solution.py:74
  232.1 6.9 %reshape.128 = bf16[1024,1792]{1,0:T(8,128)(2,1)} reshape(bf16[256,4,1792]{2,1,0:T(4,128)(2,1)} %all-gather.3.cloned.1.call-done) | data formatting | bytes 7340032
  238.9 10.4 %gather_fusion = bf16[1024,1792]{1,0:T(8,128)(2,1)} fusion(bf16[1024,1792]{1,0:T(8,128)(2,1)} %reshape.128, s32[1024]{0:T(1024)S(1)} %fusion.27), kind=kCustom, calls=%fused_computation | custom fusion | bytes 7344128 | tf_op jit(solution)/shard_map/gather | solution.py:75
  (43 shorter events, 5.6 us)
Async XLA Ops:
  8.0 92.1 %copy-start = (bf16[8,1024]{1,0:T(8,128)(2,1)S(1)}, bf16[8,1024]{1,0:T(8,128)(2,1)}, u32[]{:S(2)}) copy-start(bf16[8,1024]{1,0:T(8,128)(2,1)} %param.9) | copy-start | bytes 49156
  13.0 26.9 %all-to-all-start = ((s32[128,1,6]{2,1,0:T(1,128)}), s32[128,1,6]{2,1,0:T(1,128)S(1)}, u32[]{:S(2)}, u32[]{:S(2)}) async-start(s32[128,1,6]{2,1,0:T(1,128)} %bitcast.8), calls=%async_computation | async-start | bytes 131072 | tf_op jit(solution)/shard_map/all_to_all | solution.py:54
  39.8 56.0 %all-to-all-start.1 = ((bf16[128,6,1024]{2,1,0:T(8,128)(2,1)}), bf16[128,6,1024]{2,1,0:T(8,128)(2,1)S(1)}, u32[]{:S(2)}, u32[]{:S(2)}) async-start(bf16[128,6,1024]{2,1,0:T(8,128)(2,1)} %reshape.100), calls=%async_computation.1 | async-start | bytes 4194304 | tf_op jit(solution)/shard_map/all_to_all | solution.py:53
  46.8 75.4 %reduce-scatter.2.cloned.1.call-start = ((), (), s32[]{:S(2)}) async-start(), calls=%async_computation.3 | async-start | bytes 3145728 | tf_op jit(solution)/shard_map/reduce_scatter | solution.py:70
  48.3 51.8 %copy-start.4 = (s32[768]{0:T(1024)}, s32[768]{0:T(1024)S(1)}, u32[]{:S(2)}) copy-start(s32[768]{0:T(1024)S(1)} %eq.59) | copy-start | bytes 9220
  95.9 1.3 copy-start.1
  101.9 1.7 copy-start.2
  108.0 124.1 %all-gather.3.cloned.1.call-start = ((), (), s32[]{:S(2)}) async-start(), calls=%async_computation.4 | async-start | bytes 3684352 | tf_op jit(solution)/shard_map/all_gather | solution.py:74
  108.1 4.6 %copy-start.3 = (bf16[768,1024]{1,0:T(8,128)(2,1)S(1)}, bf16[768,1024]{1,0:T(8,128)(2,1)}, u32[]{:S(2)}) copy-start(bf16[768,1024]{1,0:T(8,128)(2,1)} %get-tuple-element.4) | copy-start | bytes 4718596
  108.1 4.6 %copy-start.5 = (s32[768]{0:T(1024)S(1)}, s32[768]{0:T(1024)}, u32[]{:S(2)}) copy-start(s32[768]{0:T(1024)} %copy-done.4) | copy-start | bytes 9220
  112.7 1.1 copy-start.7
  112.7 9.5 %copy-start.6 = (s32[1024]{0:T(1024)S(1)}, s32[1024]{0:T(1024)}, u32[]{:S(2)}) copy-start(s32[1024]{0:T(1024)} %param.8) | copy-start | bytes 12292
Sparse Core Ops, SparseCore 0:
  108.1 13.3 reduce-scatter.1
Sparse Core Ops, SparseCore 1:
  122.2 109.8 all-gather.2
where the time goes:
time: 258 us; the launch traced here: 257 us
  waiting for transfers between devices  161 us (62%)
  local copies, waits for them, and re-layouts  32.7 us (13%)
  starting transfers between devices  23.4 us (9%)
  between operations  16.4 us (6%)
  other arithmetic  10.4 us (4%)
  blocking collectives  7.53 us (3%)
  matrix products  5.58 us (2%)
    all_gather x1, waiting for transfers between devices, on_device(): table = lax.all_gather(table_part, ('dp', 'grp'), axis=0, tiled=True)  108 us
    all_to_all x1, waiting for transfers between devices, on_device(): lax.all_to_all(sent_rows, 'dp', split_axis=0, concat_axis=0, tiled=True)  47 us
    all_to_all x1, starting transfers between devices, on_device(): lax.all_to_all(sent_ids, 'dp', split_axis=0, concat_axis=0, tiled=True)  16.3 us
    unnamed x19, local copies, waits for them, and re-layouts  10.7 us
    gather x1, local copies, waits for them, and re-layouts, on_device(): shift = table[cluster_rank]  10.4 us
    unnamed x1, blocking collectives  7.53 us
    all_to_all x1, starting transfers between devices, on_device(): lax.all_to_all(sent_rows, 'dp', split_axis=0, concat_axis=0, tiled=True)  6.94 us
    all_to_all x1, waiting for transfers between devices, on_device(): lax.all_to_all(sent_ids, 'dp', split_axis=0, concat_axis=0, tiled=True)  6.3 us
  transfers between devices with their start and end apart: 4, of which 3 were waited for; matrix products, arithmetic and copies ran while one was open for 6% of the time, Pallas kernels for 0%

commit v1 on v0

--- a/solution.py
+++ b/solution.py
@@ -6,6 +6,15 @@
 D = 1024
 D_SMALL = 256
 D_MID = 512
+obtain_steps_all = lambda packet: jnp.concatenate(
+    lax.all_to_all(
+        jnp.stack([packet] * lax.axis_size(("dp", "grp")), axis=0),
+        concat_axis=0,
+        axis_name=("dp", "grp"),
+        split_axis=0,
+    ),
+    axis=0,
+)
 
 
 def residuals(rows, cent):
@@ -71,7 +80,7 @@
     )
     denom = counts_part + 1.0
     table_part = (sums_part / denom[:, None]).astype(jnp.bfloat16)
-    table = lax.all_gather(table_part, ("dp", "grp"), axis=0, tiled=True)
+    table = obtain_steps_all(table_part)
     shift = table[cluster_rank]
     moment = gram_part / denom[:, None, None]
     return (shift, moment)

time: 258 us -> 231 us (0.90)
  waiting for transfers between devices: 161 us -> 133 us
  starting transfers between devices: 23.4 us -> 30.9 us
    all_gather x1 -> x0, waiting for transfers between devices: 108 us -> none  [on_device(): table = lax.all_gather(table_part, ('dp', 'grp'), axis=0, tiled=True)]
    all_to_all x0 -> x1, waiting for transfers between devices: none -> 63.3 us  [lax.all_to_all(jnp.stack([packet] * lax.axis_size(('dp', 'grp')), axis=0)...]
    reduce_scatter x1, waiting for transfers between devices: 0.02 us -> 18 us  [on_device(): lax.psum_scatter(gram, 'grp', scatter_dimension=0, tiled=True)]
    unnamed x19 -> x16, local copies, waits for them, and re-layouts: 10.7 us -> 0.95 us
    all_to_all x0 -> x1, starting transfers between devices: none -> 7.05 us  [lax.all_to_all(jnp.stack([packet] * lax.axis_size(('dp', 'grp')), axis=0)...]
    reshape x0 -> x1, local copies, waits for them, and re-layouts: none -> 6.87 us  [jnp.concatenate(lax.all_to_all(jnp.stack([packet] * lax.axis_size(('dp',...]
    another operation x3 -> x4, local copies, waits for them, and re-layouts: 0.02 us -> 2.81 us  [the longest x1 2.79 us: jnp.stack([packet] * lax.axis_size(('dp', 'grp')), axis=0)]
  transfers between devices with their start and end apart: 4 -> 4, of which waited for: 3 -> 4; matrix products, arithmetic and copies ran while one was open for 6% -> 5% of each run, Pallas kernels for 0% -> 0%
where the time goes in v1:
time: 231 us; the launch traced here: 230 us
  waiting for transfers between devices  133 us (58%)
  local copies, waits for them, and re-layouts  31.9 us (14%)
  starting transfers between devices  30.9 us (13%)
  between operations  14.9 us (6%)
  other arithmetic  8.84 us (4%)
  blocking collectives  7.79 us (3%)
  matrix products  3.43 us (1%)
    all_to_all x1, waiting for transfers between devices, lax.all_to_all(jnp.stack([packet] * lax.axis_size(('dp', 'grp')), axis=0)...  63.3 us
    all_to_all x1, waiting for transfers between devices, on_device(): lax.all_to_all(sent_rows, 'dp', split_axis=0, concat_axis=0, tiled=True)  45.1 us
    reduce_scatter x1, waiting for transfers between devices, on_device(): lax.psum_scatter(gram, 'grp', scatter_dimension=0, tiled=True)  18 us
    all_to_all x1, starting transfers between devices, on_device(): lax.all_to_all(sent_ids, 'dp', split_axis=0, concat_axis=0, tiled=True)  16.3 us
    gather x1, local copies, waits for them, and re-layouts, on_device(): shift = table[cluster_rank]  10.4 us
    unnamed x1, blocking collectives  7.79 us
    all_to_all x1, starting transfers between devices, on_device(): lax.all_to_all(sent_rows, 'dp', split_axis=0, concat_axis=0, tiled=True)  7.49 us
    all_to_all x1, starting transfers between devices, lax.all_to_all(jnp.stack([packet] * lax.axis_size(('dp', 'grp')), axis=0)...  7.05 us
  transfers between devices with their start and end apart: 4, of which 4 were waited for; matrix products, arithmetic and copies ran while one was open for 5% of the time, Pallas kernels for 0%

profile of v1, /device:TPU:1, one launch (start us, length us, event | category | flops | bytes accessed | tf_op | source)
XLA Modules:
  0.0 230.5 jit_solution(12737741194910523419)
XLA Ops:
  7.2 0.8 copy.12
  8.3 0.9 fusion.18
  9.1 0.7 compare_select_fusion.1
  9.8 1.6 scatter_custom_fusion
  11.4 0.8 all_to_all.12
  12.2 16.3 %all-to-all-start = ((s32[128,1,6]{2,1,0:T(1,128)}), s32[128,1,6]{2,1,0:T(1,128)S(1)}, u32[]{:S(2)}, u32[]{:S(2)}) async-start(s32[128,1,6]{2,1,0:T(1,128)} %bitcast.8), calls=%async_computation | async-start | bytes 131072 | tf_op jit(solution)/shard_map/all_to_all | solution.py:63
  28.5 2.6 %scatter_custom_fusion.1 = bf16[768,1024]{1,0:T(8,128)(2,1)S(1)} fusion(s32[256]{0:T(256)S(1)} %bitcast.38, bf16[256,1024]{1,0:T(8,128)(2,1)} %param.5, bf16[]{:T(256)} %constant.7.clone.1), kind=kCustom, calls=%fused_computation.22 | custom fusion | bytes 1573376 | tf_op jit(solution)/shard_map/scatter | solution.py:57
  31.1 1.6 reshape.105
  32.7 6.3 %all-to-all-done = s32[128,1,6]{2,1,0:T(1,128)S(1)} async-done(((s32[128,1,6]{2,1,0:T(1,128)}), s32[128,1,6]{2,1,0:T(1,128)S(1)}, u32[]{:S(2)}, u32[]{:S(2)}) %all-to-all-start) | async-done | bytes 3104 | tf_op jit(solution)/shard_map/all_to_all | solution.py:63
  39.0 7.5 %all-to-all-start.1 = ((bf16[128,6,1024]{2,1,0:T(8,128)(2,1)}), bf16[128,6,1024]{2,1,0:T(8,128)(2,1)}, u32[]{:S(2)}, u32[]{:S(2)}) async-start(bf16[128,6,1024]{2,1,0:T(8,128)(2,1)} %reshape.105), calls=%async_computation.1 | async-start | bytes 4194304 | tf_op jit(solution)/shard_map/all_to_all | solution.py:62
  48.3 0.8 reduce.4
  49.2 0.6 convert_reduce_fusion
  49.9 45.1 %all-to-all-done.1 = bf16[128,6,1024]{2,1,0:T(8,128)(2,1)} async-done(((bf16[128,6,1024]{2,1,0:T(8,128)(2,1)}), bf16[128,6,1024]{2,1,0:T(8,128)(2,1)}, u32[]{:S(2)}, u32[]{:S(2)}) %all-to-all-start.1) | async-done | bytes 1572896 | tf_op jit(solution)/shard_map/all_to_all | solution.py:62
  95.0 2.5 %reshape.107 = f32[768,1024]{1,0:T(8,128)S(1)} reshape(bf16[128,6,1024]{2,1,0:T(8,128)(2,1)} %all-to-all-done.1) | data formatting | bytes 4718592 | tf_op jit(solution)/shard_map/convert_element_type | solution.py:21
  97.9 2.2 multiply_reduce_fusion
  102.2 7.8 %all-reduce.2 = (f32[8,1792]{1,0:T(8,128)S(1)}, f32[8]{0:T(128)S(1)}) all-reduce(f32[8,1792]{1,0:T(8,128)S(1)} %fusion.3, f32[8]{0:T(128)S(1)} %copy-done.5), channel_id=2, replica_groups=mesh['dp'=128,'grp'=2] {'grp'}, use_global_device_ids=true, to_apply=%region_8.9.clone | all-reduce | flops 14344 | bytes 114752
  110.2 2.8 %stack.2 = bf16[256,4,1792]{2,1,0:T(4,128)(2,1)} broadcast(bf16[4,1792]{1,0:T(4,128)(2,1)S(1)} %fusion.21), dimensions={1,2} | broadcast | bytes 3684352 | tf_op jit(solution)/shard_map/stack | solution.py:11
  113.0 7.1 %all-to-all-start.2 = ((bf16[256,4,1792]{2,1,0:T(4,128)(2,1)}), bf16[256,4,1792]{2,1,0:T(4,128)(2,1)}, u32[]{:S(2)}, u32[]{:S(2)}) async-start(bf16[256,4,1792]{2,1,0:T(4,128)(2,1)} %stack.2), calls=%async_computation.2 | async-start | bytes 7340032 | tf_op jit(solution)/shard_map/all_to_all | solution.py:10
  120.3 2.3 %fusion = f32[8,256,256]{2,1,0:T(8,128)} fusion(bf16[768,256]{0,1:T(8,128)(2,1)S(1)} %copy.15, bf16[768,8]{0,1:T(8,128)(2,1)S(1)} %fusion.22, bf16[768,256]{1,0:T(8,128)(2,1)S(1)} %fusion.12), kind=kOutput, calls=%fused_computation.4 | convolution fusion | flops 806879232 | bytes 2895872 | tf_op jit(solution)/shard_map/sa,sb->ab/dot_general | solution.py:38
  122.7 18.0 %reduce-scatter.2.cloned.1.call-done = f32[4,256,256]{2,1,0:T(8,128)} async-done(((f32[8,256,256]{2,1,0:T(8,128)}), f32[4,256,256]{2,1,0:T(8,128)}) %reduce-scatter.2.cloned.1.call-update) | async-done | bytes 1048592 | tf_op jit(solution)/shard_map/reduce_scatter | solution.py:79
  140.7 2.4 %broadcast_divide_fusion = f32[4,256,256]{2,1,0:T(8,128)} fusion(f32[4,256,256]{2,1,0:T(8,128)} %reduce-scatter.2.cloned.1.call-done, f32[4]{0:T(128)S(1)} %dynamic-slice_add_fusion), kind=kLoop, calls=%fused_computation.24 | loop fusion | flops 262144 | bytes 2097168 | tf_op jit(solution)/shard_map/div | solution.py:85
  143.0 63.3 %all-to-all-done.2 = bf16[256,4,1792]{2,1,0:T(4,128)(2,1)} async-done(((bf16[256,4,1792]{2,1,0:T(4,128)(2,1)}), bf16[256,4,1792]{2,1,0:T(4,128)(2,1)}, u32[]{:S(2)}, u32[]{:S(2)}) %all-to-all-start.2) | async-done | bytes 3670048 | tf_op jit(solution)/shard_map/all_to_all | solution.py:10
  206.3 6.9 %reshape.106 = bf16[1024,1792]{1,0:T(8,128)(2,1)} reshape(bf16[256,4,1792]{2,1,0:T(4,128)(2,1)} %all-to-all-done.2) | data formatting | bytes 7340032 | tf_op jit(solution)/shard_map/reshape | solution.py:9
  213.2 10.4 %gather_fusion = bf16[1024,1792]{1,0:T(8,128)(2,1)} fusion(bf16[1024,1792]{1,0:T(8,128)(2,1)} %reshape.106, s32[1024]{0:T(1024)S(1)} %fusion.26), kind=kCustom, calls=%fused_computation | custom fusion | bytes 7344128 | tf_op jit(solution)/shard_map/gather | solution.py:84
  (41 shorter events, 4.4 us)
Async XLA Ops:
  7.2 93.1 %copy-start = (bf16[8,1024]{1,0:T(8,128)(2,1)S(1)}, bf16[8,1024]{1,0:T(8,128)(2,1)}, u32[]{:S(2)}) copy-start(bf16[8,1024]{1,0:T(8,128)(2,1)} %param.9) | copy-start | bytes 49156
  12.2 26.9 %all-to-all-start = ((s32[128,1,6]{2,1,0:T(1,128)}), s32[128,1,6]{2,1,0:T(1,128)S(1)}, u32[]{:S(2)}, u32[]{:S(2)}) async-start(s32[128,1,6]{2,1,0:T(1,128)} %bitcast.8), calls=%async_computation | async-start | bytes 131072 | tf_op jit(solution)/shard_map/all_to_all | solution.py:63
  31.1 15.4 %copy-start.6 = (u32[256]{0:T(256)S(1)}, u32[256]{0:T(256)}, u32[]{:S(2)}) copy-start(u32[256]{0:T(256)} %constant.36) | copy-start | bytes 3076
  39.0 55.9 %all-to-all-start.1 = ((bf16[128,6,1024]{2,1,0:T(8,128)(2,1)}), bf16[128,6,1024]{2,1,0:T(8,128)(2,1)}, u32[]{:S(2)}, u32[]{:S(2)}) async-start(bf16[128,6,1024]{2,1,0:T(8,128)(2,1)} %reshape.105), calls=%async_computation.1 | async-start | bytes 4194304 | tf_op jit(solution)/shard_map/all_to_all | solution.py:62
  49.2 51.0 %copy-start.1 = (s32[768]{0:T(1024)}, s32[768]{0:T(1024)S(1)}, u32[]{:S(2)}) copy-start(s32[768]{0:T(1024)S(1)} %eq.59) | copy-start | bytes 9220
  100.9 0.7 copy-start.2
  101.6 0.6 copy-start.5
  113.0 7.1 %copy-start.3 = (s32[768]{0:T(1024)S(1)}, s32[768]{0:T(1024)}, u32[]{:S(2)}) copy-start(s32[768]{0:T(1024)} %copy-done.1) | copy-start | bytes 9220
  113.0 93.4 %all-to-all-start.2 = ((bf16[256,4,1792]{2,1,0:T(4,128)(2,1)}), bf16[256,4,1792]{2,1,0:T(4,128)(2,1)}, u32[]{:S(2)}, u32[]{:S(2)}) async-start(bf16[256,4,1792]{2,1,0:T(4,128)(2,1)} %stack.2), calls=%async_computation.2 | async-start | bytes 7340032 | tf_op jit(solution)/shard_map/all_to_all | solution.py:10
  120.0 20.7 %reduce-scatter.2.cloned.1.call-start = ((), (), s32[]{:S(2)}) async-start(), calls=%async_computation.4 | async-start | bytes 3145728 | tf_op jit(solution)/shard_map/reduce_scatter | solution.py:79
  120.3 2.4 %copy-start.4 = (s32[1024]{0:T(1024)S(1)}, s32[1024]{0:T(1024)}, u32[]{:S(2)}) copy-start(s32[1024]{0:T(1024)} %param.8) | copy-start | bytes 12292
Sparse Core Ops, SparseCore 0:
  123.3 17.3 reduce-scatter.1
